TPU v7x, 128 devices: a whole 4x4x4 slice. The times are simulated.
128 devices in a mesh: replica: 32 (over z, y, core), shard: 4 (over x).
Axes of the slice: x: 4, y: 4, z: 4, core: 2. Of those that a mesh axis runs over, the one named last changes fastest.
Arguments:
- acts: bfloat16 [2, 65536, 1280], P(None, 'replica', 'shard'), may hold values from -6 to 6
- cots: bfloat16 [2, 65536, 1280], P(None, 'replica'), may hold values from -6 to 6
- errors: float32 [32, 2, 1280, 1280], P('replica', None, 'shard'), may hold values from -4 to 4
- weights: float32 [2, 1280, 1280], P(None, 'shard'), may hold values from -0.3 to 0.3
- momentum: float32 [2, 1280, 1280], P(None, 'shard'), may hold values from -3 to 3
- start_q: float32 [2, 1280, 32], replicated, may hold values from -6 to 6
- vec_grads: float32 [32, 4, 1280], P('replica', None, 'shard'), may hold values from -6 to 6
- vec_weights: float32 [4, 1280], P(None, 'shard'), may hold values from 0.5 to 1.5
- vec_momentum: float32 [4, 1280], P(None, 'shard'), may hold values from -6 to 6
Outputs:
- new_errors: float32 [32, 2, 1280, 1280], P('replica', None, 'shard')
- new_weights: float32 [2, 1280, 1280], P(None, 'shard')
- new_momentum: float32 [2, 1280, 1280], P(None, 'shard')
- new_vec_weights: float32 [4, 1280], P(None, 'shard')
- new_vec_momentum: float32 [4, 1280], P(None, 'shard')
All inputs are finite; a program needn't handle non-finite values.
Results may differ from a plain program's by a relative error of at most 0.0003.
Values sent between devices are 32-bit elements; how exact they have to be, the bound alone decides.
No kernel may reach another device: no remote copies, remote signals or barrier semaphores. Data moves between devices by JAX's collectives and lax.ppermute only.
A program may use at most 128 MiB of HBM per device.

v0:
```python
import math
import jax
import jax.numpy as jnp
from jax import lax
from jax.sharding import PartitionSpec as P

HIGH = lax.Precision.HIGHEST


def finish(block, gram):
    lower = jnp.linalg.cholesky(gram)
    return lax.linalg.triangular_solve(lower, block, left_side=False, lower=True, transpose_a=True)


def orth_local(block):
    gram = jnp.einsum("mdk,mdl->mkl", block, block, precision=HIGH)
    return finish(block, gram)


def orth_rows(block):
    gram = jnp.einsum("mdk,mdl->mkl", block, block, precision=HIGH)
    gram = lax.psum(gram, "shard")
    return finish(block, gram)


def project_rows(full, right):
    return jnp.einsum("mde,mek->mdk", full, right, precision=HIGH)


def reduce_right(full, left):
    terms = jnp.einsum("mde,mdk->mek", full, left, precision=HIGH)
    return lax.psum(terms, ("replica", "shard"))


def body(acts, cots, errors, weights, momentum, start_q, vec_grads, vec_weights, vec_momentum):
    tok_rows = acts.shape[1]
    replicas = float(lax.axis_size("replica"))
    grads = jnp.einsum("mtd,mte->mde", acts, cots, preferred_element_type=jnp.float32)
    full = grads * (1.0 / math.sqrt(tok_rows)) + errors[0]
    local_left = project_rows(full, start_q)
    vec_total = lax.psum(vec_grads[0], "replica")
    left_sum = lax.psum(local_left, "replica")
    left = orth_rows(left_sum)
    right = reduce_right(full, left)
    right_hat = orth_local(right)
    left_sum = lax.psum(project_rows(full, right_hat), "replica")
    left = orth_rows(left_sum)
    right = reduce_right(full, left)
    approx = jnp.einsum("mdk,mek->mde", left, right, precision=HIGH) / replicas
    new_errors = (full - approx)[None]
    new_momentum = 0.9 * momentum + approx
    new_weights = weights - 0.1 * new_momentum
    vec_moved = 0.9 * vec_momentum + vec_total / replicas
    return (new_errors, new_weights, new_momentum, vec_weights - 0.1 * vec_moved, vec_moved)


def solution(mesh):
    placed = (
        P(None, "replica", "shard"),
        P(None, "replica", None),
        P("replica", None, "shard", None),
        P(None, "shard", None),
        P(None, "shard", None),
        P(),
        P("replica", None, "shard"),
        P(None, "shard"),
        P(None, "shard"),
    )
    return jax.shard_map(
        body,
        mesh=mesh,
        in_specs=placed,
        out_specs=(
            P("replica", None, "shard", None),
            P(None, "shard", None),
            P(None, "shard", None),
            P(None, "shard"),
            P(None, "shard"),
        ),
        check_vma=False,
    )
```

profile of v0, /device:TPU:1, one launch (start us, length us, event | category | flops | bytes accessed | tf_op | source)
XLA Modules:
  0.0 609.8 jit_solution(3013208280082749145)
XLA Ops:
  7.2 0.0 copy-start
  7.2 0.0 copy-start.2
  7.2 0.0 all-reduce.5.cloned.1.call-start
  7.2 1.7 copy-done
  8.9 8.5 %fusion = f32[2,320,1280]{2,1,0:T(8,128)S(1)} fusion(bf16[2,2048,320]{1,2,0:T(8,128)(2,1)S(1)} %copy-done, bf16[2,2048,1280]{2,1,0:T(8,128)(2,1)} %param.13, f32[1,2,320,1280]{3,2,1,0:T(8,128)} %param.14), kind=kOutput, calls=%fused_computation.2 | convolution fusion | flops 3357081600 | bytes 19660800 | tf_op jit(solution)/shard_map/mtd,mte->mde/dot_general | solution.py:38
  17.4 0.0 copy-start.1
  17.4 1.7 copy-done.1
  19.1 0.0 copy-done.2
  19.1 3.5 fusion.9
  22.6 0.0 all-reduce.5.cloned.1.call-update
  22.7 0.0 all-reduce.7.cloned.1.call-start
  22.7 101.0 %all-reduce.5.cloned.1.call-done = f32[2,320,32]{1,2,0:T(8,128)} async-done(((f32[2,320,32]{1,2,0:T(8,128)}), f32[2,320,32]{1,2,0:T(8,128)}) %all-reduce.5.cloned.1.call-update) | async-done | bytes 81936 | tf_op jit(solution)/shard_map/psum | solution.py:42
  123.7 1.2 fusion.10
  124.9 13.2 %psum.50 = f32[2,32,32]{1,2,0:T(8,128)S(1)} all-reduce(f32[2,32,32]{1,2,0:T(8,128)S(1)} %fusion.10), channel_id=1, replica_groups=mesh['replica'=32,'shard'=4] {'shard'}, use_global_device_ids=true, to_apply=%region_1.0 | all-reduce | flops 2048 | bytes 16384 | tf_op jit(solution)/shard_map/psum | solution.py:22
  138.2 0.1 copy.21
  138.2 5.9 custom-call.13
  144.1 0.1 compare_reduce_fusion.2
  144.3 0.1 select_bitcast_fusion.1
  144.3 4.9 custom-call.14
  149.3 1.2 convolution_bitcast_fusion.1
  150.5 4.6 fusion.11
  155.1 0.0 copy-start.3
  155.1 0.0 all-reduce.7.cloned.1.call-update
  155.1 0.2 all-reduce.9.cloned.1.call-start
  155.4 144.9 %all-reduce.7.cloned.1.call-done = f32[2,1280,32]{1,2,0:T(8,128)} async-done(((f32[2,1280,32]{1,2,0:T(8,128)}), f32[2,1280,32]{1,2,0:T(8,128)}) %all-reduce.7.cloned.1.call-update) | async-done | bytes 327696 | tf_op jit(solution)/shard_map/psum | solution.py:32
  300.3 1.5 fusion.12
  301.8 0.1 copy.22
  301.9 5.9 custom-call.15
  307.8 0.1 compare_reduce_fusion.1
  307.9 0.1 fusion.8
  308.0 4.9 custom-call.9
  312.9 1.5 fusion.3
  314.4 5.4 fusion.13
  319.8 0.0 copy-start.4
  319.8 0.0 copy-start.5
  319.8 0.0 all-reduce.9.cloned.1.call-update
  319.8 0.0 all-reduce.11.cloned.1.call-start
  319.9 0.0 copy-done.3
  319.9 62.7 %psum.55 = f32[4,320]{1,0:T(4,128)S(1)} all-reduce(f32[4,320]{1,0:T(4,128)S(1)} %bitcast.57), channel_id=1, replica_groups=mesh['replica'=32,'shard'=4] {'replica'}, use_global_device_ids=true, to_apply=%region_8.11 | all-reduce | flops 1280 | bytes 10240 | tf_op jit(solution)/shard_map/psum | solution.py:41
  382.6 32.9 %all-reduce.9.cloned.1.call-done = f32[2,320,32]{1,2,0:T(8,128)} async-done(((f32[2,320,32]{1,2,0:T(8,128)}), f32[2,320,32]{1,2,0:T(8,128)}) %all-reduce.9.cloned.1.call-update) | async-done | bytes 81936 | tf_op jit(solution)/shard_map/psum | solution.py:46
  415.5 1.2 fusion.14
  416.7 13.2 %psum.53 = f32[2,32,32]{1,2,0:T(8,128)S(1)} all-reduce(f32[2,32,32]{1,2,0:T(8,128)S(1)} %fusion.14), channel_id=1, replica_groups=mesh['replica'=32,'shard'=4] {'shard'}, use_global_device_ids=true, to_apply=%region_6.9 | all-reduce | flops 2048 | bytes 16384 | tf_op jit(solution)/shard_map/psum | solution.py:22
  430.0 0.1 copy.24
  430.1 5.9 custom-call.16
  436.0 0.1 compare_reduce_fusion
  436.1 0.1 select_bitcast_fusion
  436.2 4.9 custom-call.17
  441.1 1.2 convolution_bitcast_fusion
  442.3 4.6 fusion.15
  446.9 0.0 all-reduce.11.cloned.1.call-update
  446.9 0.0 copy-done.4
  446.9 0.0 copy-done.5
  447.0 0.6 multiply_subtract_fusion.1
  447.6 144.5 %all-reduce.11.cloned.1.call-done = f32[2,1280,32]{1,2,0:T(8,128)} async-done(((f32[2,1280,32]{1,2,0:T(8,128)}), f32[2,1280,32]{1,2,0:T(8,128)}) %all-reduce.11.cloned.1.call-update) | async-done | bytes 327696 | tf_op jit(solution)/shard_map/psum | solution.py:32
  592.0 11.3 %multiply_subtract_fusion = (f32[2,320,1280]{2,1,0:T(8,128)}, f32[2,320,1280]{2,1,0:T(8,128)}, f32[1,2,320,1280]{3,2,1,0:T(8,128)}) fusion(f32[2,320,1280]{2,1,0:T(8,128)} %param.15, f32[2,320,1280]{2,1,0:T(8,128)} %param.16, f32[2,320,1280]{2,1,0:T(8,128)} %copy-done.1, f32[2,320,32]{1,2,0:T(8,128)S(1)} %convolution_bitcast_fusion, ...), kind=kOutput, calls=%fused_computation.3 | convolution fusion | flops 319488000 | bytes 20070400 | tf_op jit(solution)/shard_map/mdk,mek->mde/dot_general | solution.py:49
  (8 shorter events, 0.1 us)
Async XLA Ops:
  7.2 1.7 copy-start
  7.2 11.9 %copy-start.2 = (f32[2,1280,32]{1,2,0:T(8,128)S(1)}, f32[2,1280,32]{1,2,0:T(8,128)}, u32[]{:S(2)}) copy-start(f32[2,1280,32]{1,2,0:T(8,128)} %param.17) | copy-start | bytes 983044
  7.2 116.5 %all-reduce.5.cloned.1.call-start = ((), (), s32[]{:S(2)}) async-start(), calls=%async_computation | async-start | bytes 196608 | tf_op jit(solution)/shard_map/psum | solution.py:42
  17.4 1.7 copy-start.1
  22.7 277.6 %all-reduce.7.cloned.1.call-start = ((), (), s32[]{:S(2)}) async-start(), calls=%async_computation.1 | async-start | bytes 655360 | tf_op jit(solution)/shard_map/psum | solution.py:32
  155.1 164.8 %copy-start.3 = (f32[1,4,320]{2,1,0:T(4,128)S(1)}, f32[1,4,320]{2,1,0:T(4,128)}, u32[]{:S(2)}) copy-start(f32[1,4,320]{2,1,0:T(4,128)} %param.18) | copy-start | bytes 15364
  155.1 260.4 %all-reduce.9.cloned.1.call-start = ((), (), s32[]{:S(2)}) async-start(), calls=%async_computation.2 | async-start | bytes 196608 | tf_op jit(solution)/shard_map/psum | solution.py:46
  319.8 127.1 %copy-start.4 = (f32[4,320]{1,0:T(4,128)S(1)}, f32[4,320]{1,0:T(4,128)}, u32[]{:S(2)}) copy-start(f32[4,320]{1,0:T(4,128)} %param.19) | copy-start | bytes 15364
  319.8 127.2 %copy-start.5 = (f32[4,320]{1,0:T(4,128)S(1)}, f32[4,320]{1,0:T(4,128)}, u32[]{:S(2)}) copy-start(f32[4,320]{1,0:T(4,128)} %param.20) | copy-start | bytes 15364
  319.8 272.2 %all-reduce.11.cloned.1.call-start = ((), (), s32[]{:S(2)}) async-start(), calls=%async_computation.3 | async-start | bytes 655360 | tf_op jit(solution)/shard_map/psum | solution.py:32
Sparse Core Ops, SparseCore 0:
  22.8 100.8 all-reduce.4
  155.2 144.9 all-reduce.6
  319.9 95.5 all-reduce.8
  447.1 144.9 all-reduce.10
where the time goes:
time: 610 us
  waiting for transfers between devices  423 us (69%)
  blocking collectives  89.2 us (15%)
  matrix products  45.7 us (7%)
  other arithmetic  33.7 us (6%)
  between operations  13.9 us (2%)
    psum x2, waiting for transfers between devices, reduce_right(): return lax.psum(terms, ('replica', 'shard'))  289 us
    psum x1, waiting for transfers between devices, body(): left_sum = lax.psum(local_left, 'replica')  101 us
    psum x1, blocking collectives, body(): vec_total = lax.psum(vec_grads[0], 'replica')  62.7 us
    psum x1, waiting for transfers between devices, body(): left_sum = lax.psum(project_rows(full, right_hat), 'replica')  32.9 us
    psum x2, blocking collectives, orth_rows(): gram = lax.psum(gram, 'shard')  26.5 us
    another operation x10, other arithmetic, finish(): lower = jnp.linalg.cholesky(gram)  18.1 us
    another operation x7, other arithmetic, finish(): lax.linalg.triangular_solve(lower, block, left_side=False, lower=True, tr...  15 us
  transfers between devices with their start and end apart: 4, of which 4 were waited for; matrix products, arithmetic and copies ran while one was open for 0% of the time, Pallas kernels for 0%

commit v1 on v0

--- a/solution.py
+++ b/solution.py
@@ -3,6 +3,7 @@
 import jax.numpy as jnp
 from jax import lax
 from jax.sharding import PartitionSpec as P
+from jax.lax import psum
 
 HIGH = lax.Precision.HIGHEST
 
@@ -29,7 +30,7 @@
 
 def reduce_right(full, left):
     terms = jnp.einsum("mde,mdk->mek", full, left, precision=HIGH)
-    return lax.psum(terms, ("replica", "shard"))
+    return psum(psum(terms, "shard"), "replica")
 
 
 def body(acts, cots, errors, weights, momentum, start_q, vec_grads, vec_weights, vec_momentum):

time: 610 us -> 636 us (1.043)
  waiting for transfers between devices: 423 us -> 444 us
    psum x1, waiting for transfers between devices: 32.9 us -> 96.9 us  [body(): left_sum = lax.psum(project_rows(full, right_hat), 'replica')]
    psum x2 -> x4, waiting for transfers between devices: 289 us -> 246 us  [reduce_right(): return psum(psum(terms, 'shard'), 'replica')]
  transfers between devices with their start and end apart: 4 -> 6, of which waited for: 4 -> 5; matrix products, arithmetic and copies ran while one was open for 0% -> 0% of each run, Pallas kernels for 0% -> 0%
where the time goes in v1:
time: 636 us
  waiting for transfers between devices  444 us (70%)
  blocking collectives  94.6 us (15%)
  matrix products  45.7 us (7%)
  other arithmetic  33.7 us (5%)
  between operations  14.3 us (2%)
    psum x4, waiting for transfers between devices, reduce_right(): return psum(psum(terms, 'shard'), 'replica')  246 us
    psum x1, waiting for transfers between devices, body(): left_sum = lax.psum(local_left, 'replica')  101 us
    psum x1, waiting for transfers between devices, body(): left_sum = lax.psum(project_rows(full, right_hat), 'replica')  96.9 us
    psum x1, blocking collectives, body(): vec_total = lax.psum(vec_grads[0], 'replica')  68.1 us
    psum x2, blocking collectives, orth_rows(): gram = lax.psum(gram, 'shard')  26.5 us
    another operation x10, other arithmetic, finish(): lower = jnp.linalg.cholesky(gram)  18.1 us
    another operation x7, other arithmetic, finish(): lax.linalg.triangular_solve(lower, block, left_side=False, lower=True, tr...  15 us
  transfers between devices with their start and end apart: 6, of which 5 were waited for; matrix products, arithmetic and copies ran while one was open for 0% of the time, Pallas kernels for 0%

profile of v1, /device:TPU:1, one launch (start us, length us, event | category | flops | bytes accessed | tf_op | source)
XLA Modules:
  0.0 635.9 jit_solution(4426941605878629004)
XLA Ops:
  7.2 0.0 copy-start
  7.2 0.0 copy-start.2
  7.2 0.0 all-reduce.7.cloned.1.call-start
  7.2 1.7 copy-done
  8.9 8.5 %fusion = f32[2,320,1280]{2,1,0:T(8,128)S(1)} fusion(bf16[2,2048,320]{1,2,0:T(8,128)(2,1)S(1)} %copy-done, bf16[2,2048,1280]{2,1,0:T(8,128)(2,1)} %param.13, f32[1,2,320,1280]{3,2,1,0:T(8,128)} %param.14), kind=kOutput, calls=%fused_computation.2 | convolution fusion | flops 3357081600 | bytes 19660800 | tf_op jit(solution)/shard_map/mtd,mte->mde/dot_general | solution.py:39
  17.4 0.0 copy-start.1
  17.4 1.7 copy-done.1
  19.1 0.0 copy-done.2
  19.1 3.5 fusion.9
  22.6 0.0 all-reduce.7.cloned.1.call-update
  22.7 0.0 all-reduce.9.cloned.1.call-start
  22.7 101.0 %all-reduce.7.cloned.1.call-done = f32[2,320,32]{1,2,0:T(8,128)} async-done(((f32[2,320,32]{1,2,0:T(8,128)}), f32[2,320,32]{1,2,0:T(8,128)}) %all-reduce.7.cloned.1.call-update) | async-done | bytes 81936 | tf_op jit(solution)/shard_map/psum | solution.py:43
  123.7 1.2 fusion.10
  124.9 13.2 %psum.64 = f32[2,32,32]{1,2,0:T(8,128)S(1)} all-reduce(f32[2,32,32]{1,2,0:T(8,128)S(1)} %fusion.10), channel_id=1, replica_groups=mesh['replica'=32,'shard'=4] {'shard'}, use_global_device_ids=true, to_apply=%region_1.0 | all-reduce | flops 2048 | bytes 16384 | tf_op jit(solution)/shard_map/psum | solution.py:23
  138.2 0.1 copy.21
  138.2 5.9 custom-call.13
  144.1 0.1 compare_reduce_fusion.2
  144.3 0.1 select_bitcast_fusion.1
  144.3 4.9 custom-call.14
  149.3 1.2 convolution_bitcast_fusion.1
  150.5 4.6 fusion.11
  155.1 0.0 all-reduce.9.cloned.1.call-update
  155.1 0.0 all-reduce.11.cloned.1.call-start
  155.2 41.4 %all-reduce.9.cloned.1.call-done = f32[2,1280,32]{1,2,0:T(8,128)} async-done(((f32[2,1280,32]{1,2,0:T(8,128)}), f32[2,1280,32]{1,2,0:T(8,128)}) %all-reduce.9.cloned.1.call-update) | async-done | bytes 327696 | tf_op jit(solution)/shard_map/psum | solution.py:33
  196.6 0.0 all-reduce.11.cloned.1.call-update
  196.6 0.2 all-reduce.13.cloned.1.call-start
  196.8 108.0 %all-reduce.11.cloned.1.call-done = f32[2,1280,32]{1,2,0:T(8,128)} async-done(((f32[2,1280,32]{1,2,0:T(8,128)}), f32[2,1280,32]{1,2,0:T(8,128)}) %all-reduce.11.cloned.1.call-update) | async-done | bytes 327696 | tf_op jit(solution)/shard_map/psum | solution.py:33
  304.8 1.5 fusion.12
  306.3 0.1 copy.22
  306.4 5.9 custom-call.15
  312.3 0.1 compare_reduce_fusion.1
  312.4 0.1 fusion.8
  312.5 4.9 custom-call.9
  317.4 1.5 fusion.3
  318.9 5.4 fusion.13
  324.3 0.0 copy-start.3
  324.3 0.0 copy-start.4
  324.3 0.0 copy-start.5
  324.3 0.0 all-reduce.13.cloned.1.call-update
  324.4 0.0 all-reduce.15.cloned.1.call-start
  324.4 96.9 %all-reduce.13.cloned.1.call-done = f32[2,320,32]{1,2,0:T(8,128)} async-done(((f32[2,320,32]{1,2,0:T(8,128)}), f32[2,320,32]{1,2,0:T(8,128)}) %all-reduce.13.cloned.1.call-update) | async-done | bytes 81936 | tf_op jit(solution)/shard_map/psum | solution.py:47
  421.3 1.2 fusion.14
  422.5 13.2 %psum.68 = f32[2,32,32]{1,2,0:T(8,128)S(1)} all-reduce(f32[2,32,32]{1,2,0:T(8,128)S(1)} %fusion.14), channel_id=1, replica_groups=mesh['replica'=32,'shard'=4] {'shard'}, use_global_device_ids=true, to_apply=%region_7.10 | all-reduce | flops 2048 | bytes 16384 | tf_op jit(solution)/shard_map/psum | solution.py:23
  435.8 0.1 copy.24
  435.9 5.9 custom-call.16
  441.8 0.1 compare_reduce_fusion
  441.9 0.1 select_bitcast_fusion
  442.0 4.9 custom-call.17
  446.9 1.2 convolution_bitcast_fusion
  448.1 4.6 fusion.15
  452.7 0.0 all-reduce.15.cloned.1.call-update
  452.7 0.0 all-reduce.17.cloned.1.call-start
  452.8 0.0 copy-done.3
  452.8 68.1 %psum.71 = f32[4,320]{1,0:T(4,128)S(1)} all-reduce(f32[4,320]{1,0:T(4,128)S(1)} %bitcast.57), channel_id=1, replica_groups=mesh['replica'=32,'shard'=4] {'replica'}, use_global_device_ids=true, to_apply=%region_10.13 | all-reduce | flops 1280 | bytes 10240 | tf_op jit(solution)/shard_map/psum | solution.py:42
  520.9 0.0 all-reduce.15.cloned.1.call-done
  520.9 0.0 all-reduce.17.cloned.1.call-update
  520.9 0.0 copy-done.4
  520.9 0.0 copy-done.5
  520.9 0.6 multiply_subtract_fusion.1
  521.6 96.2 %all-reduce.17.cloned.1.call-done = f32[2,1280,32]{1,2,0:T(8,128)} async-done(((f32[2,1280,32]{1,2,0:T(8,128)}), f32[2,1280,32]{1,2,0:T(8,128)}) %all-reduce.17.cloned.1.call-update) | async-done | bytes 327696 | tf_op jit(solution)/shard_map/psum | solution.py:33
  617.8 11.3 %multiply_subtract_fusion = (f32[2,320,1280]{2,1,0:T(8,128)}, f32[2,320,1280]{2,1,0:T(8,128)}, f32[1,2,320,1280]{3,2,1,0:T(8,128)}) fusion(f32[2,320,1280]{2,1,0:T(8,128)} %param.15, f32[2,320,1280]{2,1,0:T(8,128)} %param.16, f32[2,320,1280]{2,1,0:T(8,128)} %copy-done.1, f32[2,320,32]{1,2,0:T(8,128)S(1)} %convolution_bitcast_fusion, ...), kind=kOutput, calls=%fused_computation.3 | convolution fusion | flops 319488000 | bytes 20070400 | tf_op jit(solution)/shard_map/mdk,mek->mde/dot_general | solution.py:50
  (8 shorter events, 0.1 us)
Async XLA Ops:
  7.2 1.7 copy-start
  7.2 11.9 %copy-start.2 = (f32[2,1280,32]{1,2,0:T(8,128)S(1)}, f32[2,1280,32]{1,2,0:T(8,128)}, u32[]{:S(2)}) copy-start(f32[2,1280,32]{1,2,0:T(8,128)} %param.17) | copy-start | bytes 983044
  7.2 116.5 %all-reduce.7.cloned.1.call-start = ((), (), s32[]{:S(2)}) async-start(), calls=%async_computation | async-start | bytes 196608 | tf_op jit(solution)/shard_map/psum | solution.py:43
  17.4 1.7 copy-start.1
  22.7 173.9 %all-reduce.9.cloned.1.call-start = ((), (), s32[]{:S(2)}) async-start(), calls=%async_computation.1 | async-start | bytes 655360 | tf_op jit(solution)/shard_map/psum | solution.py:33
  155.1 149.7 %all-reduce.11.cloned.1.call-start = ((), (), s32[]{:S(2)}) async-start(), calls=%async_computation.2 | async-start | bytes 655360 | tf_op jit(solution)/shard_map/psum | solution.py:33
  196.6 224.7 %all-reduce.13.cloned.1.call-start = ((), (), s32[]{:S(2)}) async-start(), calls=%async_computation.3 | async-start | bytes 196608 | tf_op jit(solution)/shard_map/psum | solution.py:47
  324.3 128.5 %copy-start.3 = (f32[1,4,320]{2,1,0:T(4,128)S(1)}, f32[1,4,320]{2,1,0:T(4,128)}, u32[]{:S(2)}) copy-start(f32[1,4,320]{2,1,0:T(4,128)} %param.18) | copy-start | bytes 15364
  324.3 196.6 %copy-start.4 = (f32[4,320]{1,0:T(4,128)S(1)}, f32[4,320]{1,0:T(4,128)}, u32[]{:S(2)}) copy-start(f32[4,320]{1,0:T(4,128)} %param.19) | copy-start | bytes 15364
  324.3 196.6 %copy-start.5 = (f32[4,320]{1,0:T(4,128)S(1)}, f32[4,320]{1,0:T(4,128)}, u32[]{:S(2)}) copy-start(f32[4,320]{1,0:T(4,128)} %param.20) | copy-start | bytes 15364
  324.4 196.5 %all-reduce.15.cloned.1.call-start = ((), (), s32[]{:S(2)}) async-start(), calls=%async_computation.4 | async-start | bytes 655360 | tf_op jit(solution)/shard_map/psum | solution.py:33
  452.7 165.0 %all-reduce.17.cloned.1.call-start = ((), (), s32[]{:S(2)}) async-start(), calls=%async_computation.5 | async-start | bytes 655360 | tf_op jit(solution)/shard_map/psum | solution.py:33
Sparse Core Ops, SparseCore 0:
  22.8 100.8 all-reduce.6
  155.2 41.2 all-reduce.8
  200.2 104.5 all-reduce.10
  324.5 96.7 all-reduce.12
  452.9 41.2 all-reduce.14
  521.0 96.6 all-reduce.16
